TPU v7x, 128 devices: a whole 4x4x4 slice. The times are simulated.
128 devices in a mesh: row: 16 (over y, x), col: 8 (over z, core).
Axes of the slice: x: 4, y: 4, z: 4, core: 2. Of those that a mesh axis runs over, the one named last changes fastest.
Arguments:
- panel_cols: float32 [256, 16384], P('col', 'row'), as said below
- window_cols: float32 [16384, 16384], P('col', 'row'), may hold values from -6 to 6
Outputs:
- triangle: float32 [256, 256], replicated
- top_rows: float32 [16384, 256], P(('col', 'row'))
- residual: float32 [16384, 16384], P('col', 'row')
Inputs may be any that keep to these rules, and one draw needn't show every extreme that they name: `panel_cols`: the 256 rows are linearly independent over the 1024 columns of every block of row.
All inputs are finite; a program needn't handle non-finite values.
Results may differ from a plain program's by a relative error of at most 0.000084.
Values sent between devices are 32-bit elements; how exact they have to be, the bound alone decides.
A program may use at most 64 MiB of HBM per device.

v0:
```python
import jax
import jax.numpy as jnp
from jax import lax
from jax.sharding import PartitionSpec as P

precise = lax.Precision.HIGHEST


def outer_sum(left, right):
    return lax.dot_general(
        left, right, (((1,), (1,)), ((), ())), precision=precise, preferred_element_type=jnp.float32
    )


def lower_inverse(lower_part):
    identity = jnp.eye(lower_part.shape[0], dtype=jnp.float32)
    return lax.linalg.triangular_solve(lower_part, identity, left_side=True, lower=True)


def local(panel_cols, window_cols):
    slab = window_cols.shape[0]
    whole = lax.all_gather(panel_cols, "col", axis=0, tiled=True)
    cross = outer_sum(window_cols, whole)
    gram_local = outer_sum(whole, whole)
    gram_total, cross_total = lax.psum((gram_local, cross), "row")
    lower_part = jnp.linalg.cholesky(gram_total)
    inverse = lower_inverse(lower_part)
    top_all = outer_sum(cross_total, inverse)
    share_rows = slab // lax.axis_size("row")
    top_rows = lax.dynamic_slice_in_dim(top_all, lax.axis_index("row") * share_rows, share_rows, 0)
    combined = jnp.dot(top_all, inverse, precision=precise, preferred_element_type=jnp.float32)
    residual = window_cols - jnp.dot(
        combined, whole, precision=precise, preferred_element_type=jnp.float32
    )
    return (lower_part.T, top_rows, residual)


def solution(mesh):
    return jax.shard_map(
        local,
        mesh=mesh,
        in_specs=(P("col", "row"), P("col", "row")),
        out_specs=(P(), P(("col", "row"), None), P("col", "row")),
        check_vma=False,
    )
```

profile of v0, /device:TPU:0, one launch (start us, length us, event | category | flops | bytes accessed | tf_op | source)
XLA Modules:
  0.0 238.2 jit_solution(10998402472128093950)
XLA Ops:
  7.2 0.0 all-gather.2.cloned.1.call-start
  7.2 0.7 all-gather.2.cloned.1.call-update
  7.9 0.0 all-reduce.4.cloned.1.call-start
  7.9 27.7 %all-gather.2.cloned.1.call-done = f32[256,1024]{1,0:T(8,128)} async-done(((f32[32,1024]{1,0:T(8,128)}), f32[256,1024]{1,0:T(8,128)}) %all-gather.2.cloned.1.call-update) | async-done | bytes 1048592 | tf_op jit(solution)/shard_map/all_gather | solution.py:22
  35.7 3.4 %fusion.15 = f32[256,256]{0,1:T(8,128)} fusion(f32[256,1024]{1,0:T(8,128)} %all-gather.2.cloned.1.call-done), kind=kOutput, calls=%fused_computation.38 | convolution fusion | flops 805306368 | bytes 1310720 | tf_op jit(solution)/shard_map/dot_general | solution.py:10
  39.0 10.1 %fusion.16 = f32[2048,256]{1,0:T(8,128)} fusion(f32[2048,1024]{1,0:T(8,128)} %param.3, f32[256,1024]{1,0:T(8,128)S(1)} %copy-done), kind=kOutput, calls=%fused_computation.39 | convolution fusion | flops 6442450944 | bytes 11534336 | tf_op jit(solution)/shard_map/dot_general | solution.py:10
  49.2 91.9 %all-reduce.4.cloned.1.call-done = (f32[256,256]{0,1:T(8,128)}, f32[2048,256]{1,0:T(8,128)}) async-done(((f32[256,256]{0,1:T(8,128)}, f32[2048,256]{1,0:T(8,128)}), (f32[256,256]{0,1:T(8,128)}, f32[2048,256]{1,0:T(8,128)})) %all-reduce.4.cloned.1.call-update) | async-done | bytes 2359312 | tf_op jit(solution)/shard_map/psum | solution.py:25
  141.1 1.1 copy.6
  142.2 1.0 fusion
  143.2 0.7 copy-done.3
  143.9 11.7 %cholesky.50 = f32[128,128]{1,0:T(8,128)S(1)} custom-call(f32[128,128]{1,0:T(8,128)S(1)} %cholesky.118), custom_call_target="Cholesky" | custom-call | tf_op jit(solution)/shard_map/jit(cholesky)/cholesky | solution.py:26
  155.7 10.4 %custom-call.14 = f32[1,128,128]{1,2,0:T(8,128)} custom-call(f32[1,128,128]{2,1,0:T(8,128)S(1)} %get-tuple-element.31), custom_call_target="InvertDiagBlocksLowerTriangular" | custom-call | tf_op jit(solution)/shard_map/jit(cholesky)/cholesky | solution.py:26
  166.2 1.1 constant_dynamic-update-slice_fusion
  167.2 1.7 convolution_subtract_fusion.2
  169.0 12.5 %cholesky.105 = f32[128,128]{1,0:T(8,128)S(1)} custom-call(f32[128,128]{1,0:T(8,128)} %convolution_subtract_fusion.2), custom_call_target="Cholesky" | custom-call | tf_op jit(solution)/shard_map/jit(cholesky)/cholesky | solution.py:26
  181.6 0.6 compare_reduce_fusion
  183.5 1.7 fusion.1
  185.2 1.8 copy.7
  187.0 0.1 triangular_solve.44
  187.1 5.2 %while.1 = (s32[]{:T(128)}, f32[256,256]{1,0:T(8,128)S(1)}, s32[2,2]{1,0:T(2,128)S(1)}, f32[2,128,128]{2,1,0:T(8,128)}, s32[]{:T(128)}) while((s32[]{:T(128)}, f32[256,256]{1,0:T(8,128)S(1)}, s32[2,2]{1,0:T(2,128)S(1)}, f32[2,128,128]{2,1,0:T(8,128)}, s32[]{:T(128)}) %tuple.29), condition=%wide.while_cond, body=%wide.while_body.sunk | while | flops 2 | bytes 132205 | solution.py:17
  187.1 0.6 fusion.30
  187.7 2.0 bitcast_dynamic-update-slice_fusion.2
  189.7 0.6 fusion.30
  190.2 2.0 bitcast_dynamic-update-slice_fusion.2
  192.2 21.1 %custom-call.15 = f32[2,128,128]{1,2,0:T(8,128)} custom-call(f32[2,128,128]{2,1,0:T(8,128)} %get-tuple-element.10), custom_call_target="InvertDiagBlocksLowerTriangular" | custom-call | tf_op jit(solution)/shard_map/triangular_solve | solution.py:17
  213.3 1.1 fusion.5
  214.5 0.3 convolution_subtract_fusion.1
  214.7 1.2 fusion.8
  215.9 1.9 fusion.4
  217.8 1.9 fusion.3
  219.7 0.7 constant_dynamic-slice_fusion.1
  220.4 11.0 %convolution_subtract_fusion = f32[2048,1024]{1,0:T(8,128)} fusion(f32[2048,1024]{1,0:T(8,128)} %param.3, f32[2048,256]{1,0:T(8,128)S(1)} %fusion.3, f32[256,1024]{1,0:T(8,128)S(1)} %copy-done), kind=kOutput, calls=%fused_computation.2 | convolution fusion | flops 6444548096 | bytes 19922944 | tf_op jit(solution)/shard_map/dot_general | solution.py:32
  (17 shorter events, 0.2 us)
Async XLA Ops:
  7.2 28.5 %all-gather.2.cloned.1.call-start = ((), (), s32[]{:S(2)}) async-start(), calls=%async_computation | async-start | bytes 1179648 | tf_op jit(solution)/shard_map/all_gather | solution.py:22
  7.9 133.2 %all-reduce.4.cloned.1.call-start = ((), (), s32[]{:S(2)}) async-start(), calls=%async_computation.1 | async-start | bytes 4718592 | tf_op jit(solution)/shard_map/psum | solution.py:25
  35.7 3.4 %copy-start = (f32[256,1024]{1,0:T(8,128)S(1)}, f32[256,1024]{1,0:T(8,128)}, u32[]{:S(2)}) copy-start(f32[256,1024]{1,0:T(8,128)} %all-gather.2.cloned.1.call-done) | copy-start | bytes 3145732
  143.2 0.7 copy-start.3
  155.6 60.2 %copy-start.1 = (f32[2048,256]{1,0:T(8,128)S(1)}, f32[2048,256]{1,0:T(8,128)}, u32[]{:S(2)}) copy-start(f32[2048,256]{1,0:T(8,128)} %get-tuple-element.23) | copy-start | bytes 6291460
  181.6 1.9 copy-start.2
Sparse Core Ops, SparseCore 0:
  9.7 25.9 all-gather.1
  49.3 91.8 all-reduce.3
where the time goes:
time: 239 us; the launch traced here: 238 us
  waiting for transfers between devices  120 us (50%)
  other arithmetic  59.2 us (25%)
  matrix products  33.6 us (14%)
  between operations  15.5 us (6%)
  local copies, waits for them, and re-layouts  9.51 us (4%)
    psum x1, waiting for transfers between devices, local(): gram_total, cross_total = lax.psum((gram_local, cross), 'row')  91.9 us
    another operation x6, other arithmetic, local(): lower_part = jnp.linalg.cholesky(gram_total)  35.4 us
    all_gather x1, waiting for transfers between devices, local(): whole = lax.all_gather(panel_cols, 'col', axis=0, tiled=True)  27.7 us
    another operation x3, other arithmetic, lower_inverse(): lax.linalg.triangular_solve(lower_part, identity, left_side=True, lower=T...  22.8 us
    dot_general x3, matrix products, outer_sum(): lax.dot_general(left, right, (((1,), (1,)), ((), ())), precision=precise,...  15.4 us
    dot_general x1, matrix products, local(): jnp.dot(combined, whole, precision=precise, preferred_element_type=jnp.fl...  11 us
    another operation x6, local copies, waits for them, and re-layouts  5.17 us
  transfers between devices with their start and end apart: 2, of which 2 were waited for; matrix products, arithmetic and copies ran while one was open for 0% of the time, Pallas kernels for 0%

commit v1 on v0

--- a/solution.py
+++ b/solution.py
@@ -19,7 +19,9 @@
 
 def local(panel_cols, window_cols):
     slab = window_cols.shape[0]
-    whole = lax.all_gather(panel_cols, "col", axis=0, tiled=True)
+    whole = jnp.concatenate(
+        lax.all_to_all(jnp.stack([panel_cols] * lax.axis_size("col")), "col", 0, 0), axis=0
+    )
     cross = outer_sum(window_cols, whole)
     gram_local = outer_sum(whole, whole)
     gram_total, cross_total = lax.psum((gram_local, cross), "row")

time: 239 us -> 231 us (0.967)
  waiting for transfers between devices: 120 us -> 91.6 us
  blocking collectives: 0 us -> 21.2 us
    all_gather x1 -> x0, waiting for transfers between devices: 27.7 us -> none  [local(): whole = lax.all_gather(panel_cols, 'col', axis=0, tiled=True)]
    all_to_all x0 -> x1, blocking collectives: none -> 21.2 us  [local(): lax.all_to_all(jnp.stack([panel_cols] * lax.axis_size('col')), 'col', 0, 0)]
    another operation x6 -> x7, local copies, waits for them, and re-layouts: 5.17 us -> 6.15 us
  transfers between devices with their start and end apart: 2 -> 1, of which waited for: 2 -> 1; matrix products, arithmetic and copies ran while one was open for 0% -> 0% of each run, Pallas kernels for 0% -> 0%
where the time goes in v1:
time: 231 us; the launch traced here: 230 us
  waiting for transfers between devices  91.6 us (40%)
  other arithmetic  59.3 us (26%)
  matrix products  31.9 us (14%)
  blocking collectives  21.2 us (9%)
  between operations  15.4 us (7%)
  local copies, waits for them, and re-layouts  10.5 us (5%)
    psum x1, waiting for transfers between devices, local(): gram_total, cross_total = lax.psum((gram_local, cross), 'row')  91.6 us
    another operation x6, other arithmetic, local(): lower_part = jnp.linalg.cholesky(gram_total)  35.4 us
    another operation x3, other arithmetic, lower_inverse(): lax.linalg.triangular_solve(lower_part, identity, left_side=True, lower=T...  22.8 us
    all_to_all x1, blocking collectives, local(): lax.all_to_all(jnp.stack([panel_cols] * lax.axis_size('col')), 'col', 0, 0)  21.2 us
    dot_general x3, matrix products, outer_sum(): lax.dot_general(left, right, (((1,), (1,)), ((), ())), precision=precise,...  13.7 us
    dot_general x1, matrix products, local(): jnp.dot(combined, whole, precision=precise, preferred_element_type=jnp.fl...  11 us
    another operation x6, local copies, waits for them, and re-layouts  5.14 us
  transfers between devices with their start and end apart: 1, of which 1 were waited for; matrix products, arithmetic and copies ran while one was open for 0% of the time, Pallas kernels for 0%

profile of v1, /device:TPU:0, one launch (start us, length us, event | category | flops | bytes accessed | tf_op | source)
XLA Modules:
  0.0 230.0 jit_solution(1581162378213735315)
XLA Ops:
  7.2 0.0 all-reduce.4.cloned.1.call-start
  7.2 1.0 stack.2
  8.2 21.2 %all_to_all.5 = f32[8,32,1024]{2,1,0:T(8,128)S(1)} all-to-all(f32[8,32,1024]{2,1,0:T(8,128)S(1)} %stack.2), channel_id=1, replica_groups=mesh['row'=16,'col'=8] {'col'}, dimensions={0} | all-to-all | bytes 2097152 | tf_op jit(solution)/shard_map/all_to_all | solution.py:23
  29.4 1.7 fusion.15
  31.2 10.1 %fusion.16 = f32[2048,256]{1,0:T(8,128)} fusion(f32[2048,1024]{1,0:T(8,128)} %param.3, f32[256,1024]{1,0:T(8,128)S(1)} %bitcast.43), kind=kOutput, calls=%fused_computation.39 | convolution fusion | flops 6442450944 | bytes 11534336 | tf_op jit(solution)/shard_map/dot_general | solution.py:10
  41.2 0.0 all-reduce.4.cloned.1.call-update
  41.3 91.6 %all-reduce.4.cloned.1.call-done = (f32[256,256]{0,1:T(8,128)}, f32[2048,256]{1,0:T(8,128)}) async-done(((f32[256,256]{0,1:T(8,128)}, f32[2048,256]{1,0:T(8,128)}), (f32[256,256]{0,1:T(8,128)}, f32[2048,256]{1,0:T(8,128)})) %all-reduce.4.cloned.1.call-update) | async-done | bytes 2359312 | tf_op jit(solution)/shard_map/psum | solution.py:27
  132.9 1.1 copy.6
  134.0 1.0 fusion
  135.0 0.7 copy-done.2
  135.7 11.7 %cholesky.50 = f32[128,128]{1,0:T(8,128)S(1)} custom-call(f32[128,128]{1,0:T(8,128)S(1)} %cholesky.118), custom_call_target="Cholesky" | custom-call | tf_op jit(solution)/shard_map/jit(cholesky)/cholesky | solution.py:28
  147.4 10.4 %custom-call.14 = f32[1,128,128]{1,2,0:T(8,128)} custom-call(f32[1,128,128]{2,1,0:T(8,128)S(1)} %get-tuple-element.31), custom_call_target="InvertDiagBlocksLowerTriangular" | custom-call | tf_op jit(solution)/shard_map/jit(cholesky)/cholesky | solution.py:28
  157.9 1.1 constant_dynamic-update-slice_fusion
  159.0 1.7 convolution_subtract_fusion.2
  160.7 12.5 %cholesky.105 = f32[128,128]{1,0:T(8,128)S(1)} custom-call(f32[128,128]{1,0:T(8,128)} %convolution_subtract_fusion.2), custom_call_target="Cholesky" | custom-call | tf_op jit(solution)/shard_map/jit(cholesky)/cholesky | solution.py:28
  173.3 0.7 compare_reduce_fusion
  175.3 1.7 fusion.1
  177.0 1.8 copy.7
  178.8 0.1 triangular_solve.44
  178.8 5.1 %while.1 = (s32[]{:T(128)}, f32[256,256]{1,0:T(8,128)S(1)}, s32[2,2]{1,0:T(2,128)S(1)}, f32[2,128,128]{2,1,0:T(8,128)}, s32[]{:T(128)}) while((s32[]{:T(128)}, f32[256,256]{1,0:T(8,128)S(1)}, s32[2,2]{1,0:T(2,128)S(1)}, f32[2,128,128]{2,1,0:T(8,128)}, s32[]{:T(128)}) %tuple.29), condition=%wide.while_cond, body=%wide.while_body.sunk | while | flops 2 | bytes 132205 | solution.py:17
  178.8 0.6 fusion.30
  179.4 2.0 bitcast_dynamic-update-slice_fusion.2
  181.4 0.6 fusion.30
  182.0 2.0 bitcast_dynamic-update-slice_fusion.2
  184.0 21.1 %custom-call.15 = f32[2,128,128]{1,2,0:T(8,128)} custom-call(f32[2,128,128]{2,1,0:T(8,128)} %get-tuple-element.10), custom_call_target="InvertDiagBlocksLowerTriangular" | custom-call | tf_op jit(solution)/shard_map/triangular_solve | solution.py:17
  205.1 1.1 fusion.5
  206.2 0.3 convolution_subtract_fusion.1
  206.5 1.1 fusion.8
  207.6 1.9 fusion.4
  209.6 1.9 fusion.3
  211.5 0.7 constant_dynamic-slice_fusion.1
  212.1 11.0 %convolution_subtract_fusion = f32[2048,1024]{1,0:T(8,128)} fusion(f32[2048,1024]{1,0:T(8,128)} %param.3, f32[2048,256]{1,0:T(8,128)S(1)} %fusion.3, f32[256,1024]{1,0:T(8,128)S(1)} %bitcast.44), kind=kOutput, calls=%fused_computation.2 | convolution fusion | flops 6444548096 | bytes 19922944 | tf_op jit(solution)/shard_map/dot_general | solution.py:34
  (14 shorter events, 0.2 us)
Async XLA Ops:
  7.2 125.7 %all-reduce.4.cloned.1.call-start = ((), (), s32[]{:S(2)}) async-start(), calls=%async_computation.1 | async-start | bytes 4718592 | tf_op jit(solution)/shard_map/psum | solution.py:27
  135.0 0.7 copy-start.2
  147.4 60.2 %copy-start = (f32[2048,256]{1,0:T(8,128)S(1)}, f32[2048,256]{1,0:T(8,128)}, u32[]{:S(2)}) copy-start(f32[2048,256]{1,0:T(8,128)} %get-tuple-element.23) | copy-start | bytes 6291460
  173.3 1.9 copy-start.1
Sparse Core Ops, SparseCore 0:
  41.4 91.4 all-reduce.3
